TPU v7x, 256 devices: a whole 4x4x8 slice. The times are simulated.
256 devices in a mesh: sta: 64 (over x_lo, z, y), tpl: 4 (over x_hi, core).
Axes of the slice: x: 4 (x_hi: 2, x_lo: 2; x = x_hi * 2 + x_lo), y: 4, z: 8, core: 2. Of those that a mesh axis runs over, the one named last changes fastest.
Arguments:
- waveform: float32 [128, 1536], P('sta', 'tpl'), may hold values from -6 to 6
- fir_taps: float32 [64], replicated, may hold values from -0.75 to 0.75
- templates: bfloat16 [512, 128, 1024], P('tpl', 'sta'), may hold values from -6 to 6
- presence: int32 [512, 128], P('tpl', 'sta'), may hold values from 0 to 1
- moveout: int32 [512, 128], P('tpl', 'sta'), may hold values from 0 to 128
Outputs:
- network_stack: float32 [4, 128, 384], P('tpl', 'sta')
All inputs are finite; a program needn't handle non-finite values.
Results may differ from a plain program's by a relative error of at most 0.0029.
Values may be sent and summed in bfloat16 or wider, within the bound.
A program may use at most 64 MiB of HBM per device.

v0:
```python
import jax
import jax.numpy as jnp
from jax import lax
from jax.sharding import PartitionSpec as P

BLK = 128
SHIFT_MOST = 128
epsilon = 1e-06


def fir_apply(extended, coeffs):
    result = lax.conv_general_dilated(
        extended[:, None, :],
        coeffs[::-1][None, None, :],
        (1,),
        "VALID",
        precision=lax.Precision.HIGHEST,
    )
    return result[:, 0, :]


def hankel(samples):
    leading = samples.shape[:-1]
    row_total = samples.shape[-1] // BLK
    row_blocks = samples.reshape(leading + (row_total, BLK))
    windows = jnp.concatenate([row_blocks[..., :-1, :], row_blocks[..., 1:, :]], axis=-1)
    tiled_win = jnp.tile(windows, (1,) * (windows.ndim - 1) + (BLK + 1,))
    flat_win = tiled_win[..., : BLK * (2 * BLK + 1)]
    return flat_win.reshape(windows.shape[:-1] + (BLK, 2 * BLK + 1))[..., :BLK]


def shards(waveform, fir_taps, templates, presence, moveout):
    tap_count = fir_taps.shape[0]
    gathered = lax.all_gather(waveform, "tpl", axis=1, tiled=True)
    extended = jnp.pad(gathered, ((0, 0), (tap_count - 1, 0)))
    filtered = fir_apply(extended, fir_taps).astype(jnp.bfloat16)
    station_count = filtered.shape[0]
    templ_len = templates.shape[2]
    block_rows = templates.shape[0]
    corr_len = filtered.shape[1] - templ_len
    out_len = corr_len - SHIFT_MOST
    time_blocks = corr_len // BLK
    lag_blocks = templ_len // BLK
    values = filtered.astype(jnp.float32)
    prefix = jnp.concatenate(
        [jnp.zeros((station_count, 1), jnp.float32), jnp.cumsum(values * values, axis=1)], axis=1
    )
    energy = prefix[:, templ_len : templ_len + corr_len] - prefix[:, :corr_len]
    root_energy = jnp.sqrt(energy)
    hankel_rows = hankel(filtered)
    templ_norm = jnp.sqrt(jnp.sum(jnp.square(templates.astype(jnp.float32)), axis=-1) + epsilon)
    lag_index = jnp.arange(out_len, dtype=jnp.int32)
    own_rows = block_rows // lax.axis_size("sta")
    templ_split = templates.reshape(block_rows, station_count, lag_blocks, BLK)
    products = jnp.zeros((station_count, block_rows, time_blocks, BLK), jnp.float32)
    for offset in range(lag_blocks):
        products = products + jnp.einsum(
            "ksb,scbd->skcd",
            templ_split[:, :, offset, :],
            hankel_rows[:, offset : offset + time_blocks],
            preferred_element_type=jnp.float32,
        )
    products = products.reshape(station_count, block_rows, corr_len)
    correlation = products / (templ_norm.T[:, :, None] * root_energy[:, None, :])
    shifts = moveout.T
    weights = presence.T.astype(jnp.float32)
    positions = shifts[:, :, None] + lag_index[None, None, :]
    aligned = jnp.take_along_axis(correlation, positions, axis=2)
    summed = lax.psum(jnp.sum(weights[:, :, None] * aligned, axis=0), "sta")
    dev_index = lax.axis_index("sta")
    stacked = lax.dynamic_slice_in_dim(summed, dev_index * own_rows, own_rows, 0)
    return stacked[None]


def solution(mesh):
    placed = (P("sta", "tpl"), P(), P("tpl", "sta", None), P("tpl", "sta"), P("tpl", "sta"))
    return jax.shard_map(
        shards, mesh=mesh, in_specs=placed, out_specs=P("tpl", "sta", None), check_vma=False
    )
```

profile of v0, /device:TPU:6, one launch (start us, length us, event | category | flops | bytes accessed | tf_op | source)
XLA Modules:
  0.0 1396.6 jit_solution(3931908676046544148)
XLA Ops:
  6.5 6.8 all_gather.3
  13.3 0.1 pad_bitcast_fusion
  13.4 0.1 reshape.59
  13.5 0.1 fusion.15
  13.6 0.1 copy.74
  13.7 0.8 rev.3
  14.5 0.1 copy.75
  14.6 15.2 %fusion.20 = bf16[16,200,1]{0,2,1:T(2,128)(2,1)S(1)} fusion(f32[1,16,263]{1,0,2:T(1,128)S(1)} %copy.74, f32[1,1,64]{1,0,2:T(1,128)S(1)} %copy.75), kind=kOutput, calls=%fused_computation.54 | convolution fusion | flops 2457600 | bytes 23488 | tf_op jit(solution)/shard_map/conv_general_dilated | solution.py:12
  29.9 0.1 copy.76
  30.0 0.1 reshape.63
  30.1 0.0 copy-done
  30.1 0.7 copy.79
  30.9 1.2 multiply_reduce_fusion
  32.1 0.1 tile.4
  32.2 2.2 tile.10
  34.5 2.1 slice.110
  36.6 6.0 reshape.53
  42.6 0.0 copy-start.6
  42.6 1.4 fusion.18
  44.0 0.6 reduce-window.6
  44.6 0.2 slice_reduce_fusion
  44.7 0.2 reduce-window.9
  44.9 0.1 add_bitcast_fusion
  45.0 0.1 fusion.17
  45.1 0.9 sqrt_bitcast_fusion
  46.0 0.1 copy.95
  46.0 0.2 fusion.2
  46.3 0.3 fusion.13
  46.6 0.3 convolution_add_fusion.6
  46.9 0.0 copy-start.1
  46.9 0.0 copy-done.4
  46.9 0.3 convolution_add_fusion.5
  47.2 0.0 copy-done.3
  47.2 0.3 convolution_add_fusion.4
  47.5 0.1 copy-done.2
  47.6 0.3 convolution_add_fusion.3
  47.8 0.0 copy-done.1
  47.9 0.3 convolution_add_fusion.2
  48.2 0.3 convolution_add_fusion.1
  48.5 0.3 convolution_add_fusion
  48.7 0.2 bitcast_divide_fusion
  49.0 0.0 copy-start.8
  49.0 787.1 %gather_fusion = f32[98304]{0:T(1024)S(1)} fusion(f32[2,128,512]{1,2,0:T(8,128)S(1)} %bitcast_divide_fusion, s32[98304]{0:T(1024)S(1)} %reshape.72), kind=kCustom, calls=%fused_computation | custom fusion | bytes 1966080 | tf_op jit(solution)/shard_map/jit(take_along_axis)/gather | solution.py:68
  836.1 0.1 reshape.75
  836.2 0.9 multiply_reduce_fusion.1
  837.1 0.0 all-reduce.4.cloned.1.call-update
  837.1 551.3 %all-reduce.4.cloned.1.call-done = f32[128,384]{1,0:T(8,128)} async-done(((f32[128,384]{1,0:T(8,128)}), f32[128,384]{1,0:T(8,128)}) %all-reduce.4.cloned.1.call-update) | async-done | bytes 196624 | tf_op jit(solution)/shard_map/psum | solution.py:69
  1388.4 1.3 dynamic-slice_bitcast_fusion
  (23 shorter events, 0.1 us)
Async XLA Ops:
  6.5 1381.9 %all-reduce.4.cloned.1.call-start = ((), (), s32[]{:S(2)}) async-start(), calls=%async_computation | async-start | bytes 393216 | tf_op jit(solution)/shard_map/psum | solution.py:69
  14.6 15.3 %copy-start.7 = (pred[16,200,1]{1,0,2:T(8,128)(4,1)S(1)}, pred[16,200,1]{1,0,2:T(8,128)(4,1)}, u32[]{:S(2)}) copy-start(pred[16,200,1]{1,0,2:T(8,128)(4,1)} %constant.49) | copy-start | bytes 9604
  14.6 15.5 %copy-start = (bf16[128,2,1024]{2,1,0:T(2,128)(2,1)S(1)}, bf16[128,2,1024]{2,1,0:T(2,128)(2,1)}, u32[]{:S(2)}) copy-start(bf16[128,2,1024]{2,1,0:T(2,128)(2,1)} %param.7) | copy-start | bytes 1572868
  42.6 3.4 copy-start.6
  44.0 2.6 copy-start.5
  44.0 2.9 copy-start.4
  46.3 1.0 copy-start.3
  46.6 1.0 copy-start.2
  46.9 1.0 copy-start.1
  49.0 787.2 %copy-start.8 = (s32[128,2]{0,1:T(2,128)S(1)}, s32[128,2]{0,1:T(2,128)}, u32[]{:S(2)}) copy-start(s32[128,2]{0,1:T(2,128)} %param.8) | copy-start | bytes 3076
Sparse Core Ops, SparseCore 0:
  837.3 551.1 all-reduce.3
where the time goes:
time: 1400 us
  local copies, waits for them, and re-layouts  803 us (57%)
  waiting for transfers between devices  551 us (39%)
  matrix products  17.5 us (1%)
    gather x3, local copies, waits for them, and re-layouts, shards(): aligned = jnp.take_along_axis(correlation, positions, axis=2)  787 us
    psum x1, waiting for transfers between devices, shards(): summed = lax.psum(jnp.sum(weights[:, :, None] * aligned, axis=0), 'sta')  551 us
  transfers between devices with their start and end apart: 1, of which 1 were waited for; matrix products, arithmetic and copies ran while one was open for 0% of the time, Pallas kernels for 0%

commit v1 on v0

--- a/solution.py
+++ b/solution.py
@@ -66,7 +66,7 @@
     weights = presence.T.astype(jnp.float32)
     positions = shifts[:, :, None] + lag_index[None, None, :]
     aligned = jnp.take_along_axis(correlation, positions, axis=2)
-    summed = lax.psum(jnp.sum(weights[:, :, None] * aligned, axis=0), "sta")
+    summed = jnp.sum(lax.all_gather(jnp.sum(weights[:, :, None] * aligned, axis=0), "sta"), axis=0)
     dev_index = lax.axis_index("sta")
     stacked = lax.dynamic_slice_in_dim(summed, dev_index * own_rows, own_rows, 0)
     return stacked[None]

time: 1400 us -> 1180 us (0.84)
  waiting for transfers between devices: 551 us -> 323 us
    psum x1 -> x0, waiting for transfers between devices: 551 us -> none  [shards(): summed = lax.psum(jnp.sum(weights[:, :, None] * aligned, axis=0), 'sta')]
    all_gather x0 -> x1, waiting for transfers between devices: none -> 323 us  [shards(): lax.all_gather(jnp.sum(weights[:, :, None] * aligned, axis=0), 'sta')]
where the time goes in v1:
time: 1180 us
  local copies, waits for them, and re-layouts  802 us (68%)
  waiting for transfers between devices  323 us (27%)
  matrix products  22.2 us (2%)
  between operations  13.6 us (1%)
    gather x3, local copies, waits for them, and re-layouts, shards(): aligned = jnp.take_along_axis(correlation, positions, axis=2)  787 us
    all_gather x1, waiting for transfers between devices, shards(): lax.all_gather(jnp.sum(weights[:, :, None] * aligned, axis=0), 'sta')  323 us
  transfers between devices with their start and end apart: 1, of which 1 were waited for; matrix products, arithmetic and copies ran while one was open for 0% of the time, Pallas kernels for 0%

profile of v1, /device:TPU:6, one launch (start us, length us, event | category | flops | bytes accessed | tf_op | source)
XLA Modules:
  0.0 1177.4 jit_solution(12378571498583046298)
XLA Ops:
  6.5 0.0 copy-start.2
  6.5 0.0 all-gather.3.cloned.1.call-start
  6.5 6.9 all_gather.9
  13.5 0.1 pad_bitcast_fusion
  13.6 0.1 reshape.59
  13.7 0.1 fusion.15
  13.8 0.1 copy.74
  13.9 0.8 rev.3
  14.6 0.1 copy.75
  14.7 15.2 %fusion.20 = bf16[16,200,1]{0,2,1:T(2,128)(2,1)S(1)} fusion(f32[1,16,263]{1,0,2:T(1,128)S(1)} %copy.74, f32[1,1,64]{1,0,2:T(1,128)S(1)} %copy.75), kind=kOutput, calls=%fused_computation.54 | convolution fusion | flops 2457600 | bytes 23488 | tf_op jit(solution)/shard_map/conv_general_dilated | solution.py:12
  30.0 0.1 copy.76
  30.0 0.0 copy-done.2
  30.1 0.1 reshape.63
  30.2 0.0 copy-done
  30.2 0.7 copy.79
  31.0 1.2 multiply_reduce_fusion
  32.2 0.1 tile.4
  32.4 2.2 tile.10
  34.6 2.1 slice.110
  36.7 6.0 reshape.53
  42.7 1.4 fusion.18
  44.1 0.6 reduce-window.6
  44.7 0.2 slice_reduce_fusion
  44.8 0.2 reduce-window.9
  45.0 0.1 add_bitcast_fusion
  45.1 0.1 fusion.17
  45.2 0.9 sqrt_bitcast_fusion
  46.1 0.1 copy.95
  46.1 0.0 copy-done.1
  46.1 0.2 fusion.2
  46.4 0.3 fusion.13
  46.7 1.2 convolution_add_fusion.6
  47.9 1.2 convolution_add_fusion.5
  49.2 1.2 convolution_add_fusion.4
  50.4 1.2 convolution_add_fusion.3
  51.6 1.2 convolution_add_fusion.2
  52.9 0.3 convolution_add_fusion.1
  53.2 0.3 convolution_add_fusion
  53.5 0.2 bitcast_divide_fusion
  53.7 0.0 copy-start.3
  53.7 787.1 %gather_fusion = f32[98304]{0:T(1024)S(1)} fusion(f32[2,128,512]{1,2,0:T(8,128)S(1)} %bitcast_divide_fusion, s32[98304]{0:T(1024)S(1)} %reshape.72), kind=kCustom, calls=%fused_computation | custom fusion | bytes 1966080 | tf_op jit(solution)/shard_map/jit(take_along_axis)/gather | solution.py:68
  840.8 0.1 reshape.75
  840.9 0.0 copy-done.3
  840.9 0.9 multiply_reduce_fusion.1
  841.8 0.0 all-gather.3.cloned.1.call-update
  841.9 322.9 %all-gather.3.cloned.1.call-done = f32[8192,384]{1,0:T(8,128)} async-done(((f32[128,384]{1,0:T(8,128)}), f32[8192,384]{1,0:T(8,128)}) %all-gather.3.cloned.1.call-update) | async-done | bytes 12582928 | tf_op jit(solution)/shard_map/all_gather | solution.py:69
  1164.8 5.2 reduce_sum.29
  1169.9 0.6 dynamic-slice_bitcast_fusion
  (14 shorter events, 0.1 us)
Async XLA Ops:
  6.5 23.5 %copy-start.2 = (pred[16,200,1]{1,0,2:T(8,128)(4,1)S(1)}, pred[16,200,1]{1,0,2:T(8,128)(4,1)}, u32[]{:S(2)}) copy-start(pred[16,200,1]{1,0,2:T(8,128)(4,1)} %constant.49) | copy-start | bytes 9604
  6.5 23.7 %copy-start = (bf16[128,2,1024]{2,1,0:T(2,128)(2,1)S(1)}, bf16[128,2,1024]{2,1,0:T(2,128)(2,1)}, u32[]{:S(2)}) copy-start(bf16[128,2,1024]{2,1,0:T(2,128)(2,1)} %param.7) | copy-start | bytes 1572868
  6.5 1158.2 %all-gather.3.cloned.1.call-start = ((), (), s32[]{:S(2)}) async-start(), calls=%async_computation | async-start | bytes 12779520 | tf_op jit(solution)/shard_map/all_gather | solution.py:69
  30.0 16.2 %copy-start.1 = (s32[128,2]{0,1:T(2,128)S(1)}, s32[128,2]{0,1:T(2,128)}, u32[]{:S(2)}) copy-start(s32[128,2]{0,1:T(2,128)} %param.9) | copy-start | bytes 3076
  53.7 787.2 %copy-start.3 = (s32[128,2]{0,1:T(2,128)S(1)}, s32[128,2]{0,1:T(2,128)}, u32[]{:S(2)}) copy-start(s32[128,2]{0,1:T(2,128)} %param.8) | copy-start | bytes 3076
Sparse Core Ops, SparseCore 0:
  842.0 322.7 all-gather.2
